TPU v7x, 32 devices: a whole 2x2x4 slice. The times are simulated.
32 devices in a mesh: fsdp: 16 (over z, x, core), tensor: 2 (over y).
Axes of the slice: x: 2, y: 2, z: 4, core: 2. Of those that a mesh axis runs over, the one named last changes fastest.
Arguments:
- tokens: bfloat16 [8192, 1024], P(('fsdp', 'tensor')), may hold values from -6 to 6
- segments: int32 [16, 512], P('fsdp'), may hold values from 0 to 3, never falling along the last dimension, each value on 1 to 256 neighbouring positions
- norm_gains: float32 [2, 1024], P(None, ('fsdp', 'tensor')), may hold values from 0.5 to 1.5
- row_biases: float32 [4, 1024], P(None, ('fsdp', 'tensor')), may hold values from -3 to 3
- attention_in: bfloat16 [1024, 3, 1024], P('fsdp', None, 'tensor'), may hold values from -0.1875 to 0.1875
- query_bias: bfloat16 [16, 64], P('tensor', 'fsdp'), may hold values from -3 to 3
- value_bias: bfloat16 [16, 64], P('tensor', 'fsdp'), may hold values from -1.1953125 to 1.1953125
- attention_out: bfloat16 [1024, 1024], P('tensor', 'fsdp'), may hold values from -0.75 to 0.75
- hidden_in: bfloat16 [1024, 4096], P('fsdp', 'tensor'), may hold values from -0.1875 to 0.1875
- hidden_bias: bfloat16 [16, 256], P('tensor', 'fsdp'), may hold values from -3 to 3
- hidden_out: bfloat16 [4096, 1024], P('tensor', 'fsdp'), may hold values from -0.09375 to 0.09375
- output_grad: bfloat16 [8192, 1024], P(('fsdp', 'tensor')), may hold values from -6 to 6
Outputs:
- output: bfloat16 [8192, 1024], P(('fsdp', 'tensor'))
- tokens_grad: bfloat16 [8192, 1024], P(('fsdp', 'tensor'))
- attention_in_grad: float32 [1024, 3, 1024], P('fsdp', None, 'tensor')
- attention_out_grad: float32 [1024, 1024], P('tensor', 'fsdp')
- hidden_in_grad: float32 [1024, 4096], P('fsdp', 'tensor')
- hidden_out_grad: float32 [4096, 1024], P('tensor', 'fsdp')
- query_bias_grad: float32 [16, 64], P('tensor', 'fsdp')
- value_bias_grad: float32 [16, 64], P('tensor', 'fsdp')
- hidden_bias_grad: float32 [16, 256], P('tensor', 'fsdp')
- norm_gains_grad: float32 [2, 1024], P(None, ('fsdp', 'tensor'))
- row_biases_grad: float32 [4, 1024], P(None, ('fsdp', 'tensor'))
Inputs may be any that keep to these rules, and one draw needn't show every extreme that they name: `segments`: along each sequence segment numbers never fall; each sequence holds documents of 1 to 256 tokens, one of exactly 256.
All inputs are finite; a program needn't handle non-finite values.
Results may differ from a plain program's by a relative error of at most 0.017.
Values may be sent and summed in bfloat16 or wider, within the bound.
No kernel may reach another device: no remote copies, remote signals or barrier semaphores. Data moves between devices by JAX's collectives and lax.ppermute only.
A program may use at most 128 MiB of HBM per device.

v0:
```python
import math

import jax
import jax.numpy as jnp
from jax import lax
from jax.sharding import PartitionSpec as P

HD = 64


EPS = 1e-05
GELU_C = math.sqrt(2.0 / math.pi)
GELU_A = 0.044715
MASKED = -1e30


def gelu_value(pre_act):
    return (
        0.5 * pre_act * (1.0 + jnp.tanh(GELU_C * (pre_act + GELU_A * pre_act * pre_act * pre_act)))
    )


def gelu_slope(pre_act):
    tanh_part = jnp.tanh(GELU_C * (pre_act + GELU_A * pre_act * pre_act * pre_act))
    return 0.5 * (1.0 + tanh_part) + 0.5 * pre_act * (1.0 - tanh_part * tanh_part) * GELU_C * (
        1.0 + 3.0 * GELU_A * pre_act * pre_act
    )


def normalize(row_data, gain_row, shift_row):
    row_mean = jnp.mean(row_data, axis=-1, keepdims=True)
    centered = row_data - row_mean
    variance = jnp.mean(centered * centered, axis=-1, keepdims=True)
    inverse = lax.rsqrt(variance + EPS)
    normed = centered * inverse
    return (normed * gain_row + shift_row, normed, inverse)


def normalize_back(grad_rows, normed, inverse, gain_row):
    scaled = grad_rows * gain_row
    return inverse * (
        scaled
        - jnp.mean(scaled, axis=-1, keepdims=True)
        - normed * jnp.mean(scaled * normed, axis=-1, keepdims=True)
    )


def pair_mask(segments):
    places = jnp.arange(segments.shape[1])
    causal = places[:, None] >= places[None, :]
    same_doc = segments[:, :, None] == segments[:, None, :]
    return (causal[None] & same_doc)[:, None]


def head_scores(query_rows, key_rows, allowed, score_scale):
    scores = (
        jnp.einsum("sqhe,skhe->shqk", query_rows, key_rows, preferred_element_type=jnp.float32)
        * score_scale
    )
    return jnp.where(allowed, scores, MASKED)


def spread_rows(local_rows):
    return lax.all_gather(local_rows, "tensor", axis=0, tiled=True)


def collect_rows(partial_rows):
    return lax.psum_scatter(
        partial_rows.astype(jnp.bfloat16), "tensor", scatter_dimension=0, tiled=True
    ).astype(jnp.float32)


def spread_grads(local_rows):
    return lax.all_gather(local_rows, "tensor", axis=0, tiled=True)


def collect_grads(partial_rows):
    return lax.psum_scatter(
        partial_rows.astype(jnp.bfloat16), "tensor", scatter_dimension=0, tiled=True
    ).astype(jnp.float32)


def shards(
    tokens,
    segments,
    norm_gains,
    row_biases,
    attention_in,
    query_bias,
    value_bias,
    attention_out,
    hidden_in,
    hidden_bias,
    hidden_out,
    output_grad,
):
    forward_set = (
        lax.all_gather(attention_in, "fsdp", axis=0, tiled=True),
        lax.all_gather(attention_out, "fsdp", axis=1, tiled=True),
        lax.all_gather(hidden_in, "fsdp", axis=0, tiled=True),
        lax.all_gather(hidden_out, "fsdp", axis=1, tiled=True),
        lax.all_gather(query_bias, "fsdp", axis=1, tiled=True),
        lax.all_gather(value_bias, "fsdp", axis=1, tiled=True),
        lax.all_gather(hidden_bias, "fsdp", axis=1, tiled=True),
    )
    gains_all, biases_all = (
        lax.all_gather(norm_gains, ("fsdp", "tensor"), axis=1, tiled=True),
        lax.all_gather(row_biases, ("fsdp", "tensor"), axis=1, tiled=True),
    )
    in_full, out_full, up_full, down_full, query_add, value_add, hidden_add = forward_set
    model_width = in_full.shape[0]
    local_width = in_full.shape[2]
    seq_count = segments.shape[0]
    seq_len = segments.shape[1]
    head_shape = (seq_count, seq_len, local_width // HD, HD)
    score_scale = 1.0 / math.sqrt(HD)
    allowed = pair_mask(segments)
    tok_rows = tokens.astype(jnp.float32)
    norm_one, normed_one, inverse_one = normalize(tok_rows, gains_all[0], biases_all[0])
    in_one = spread_rows(norm_one.astype(jnp.bfloat16))
    projected = jnp.dot(
        in_one, in_full.reshape(model_width, 3 * local_width), preferred_element_type=jnp.float32
    ).reshape(-1, 3, local_width)
    query_rows = (
        (projected[:, 0] + query_add.reshape(local_width).astype(jnp.float32))
        .astype(jnp.bfloat16)
        .reshape(head_shape)
    )
    key_rows = projected[:, 1].astype(jnp.bfloat16).reshape(head_shape)
    value_rows = (
        (projected[:, 2] + value_add.reshape(local_width).astype(jnp.float32))
        .astype(jnp.bfloat16)
        .reshape(head_shape)
    )
    scores = head_scores(query_rows, key_rows, allowed, score_scale)
    row_top = jnp.max(scores, axis=-1, keepdims=True)
    exp_terms = jnp.exp(scores - row_top)
    exp_total = jnp.sum(exp_terms, axis=-1, keepdims=True)
    log_total = row_top + jnp.log(exp_total)
    probs_b = (exp_terms / exp_total).astype(jnp.bfloat16)
    mixed = jnp.einsum("shqk,skhe->sqhe", probs_b, value_rows, preferred_element_type=jnp.float32)
    mixed_rows = mixed.reshape(-1, local_width).astype(jnp.bfloat16)
    attn_rows = collect_rows(jnp.dot(mixed_rows, out_full, preferred_element_type=jnp.float32))
    resid_rows = tok_rows + attn_rows + biases_all[1]
    norm_two, normed_two, inverse_two = normalize(resid_rows, gains_all[1], biases_all[2])
    in_two = spread_rows(norm_two.astype(jnp.bfloat16))
    pre_act = jnp.dot(in_two, up_full, preferred_element_type=jnp.float32) + hidden_add.reshape(
        -1
    ).astype(jnp.float32)
    act_rows = gelu_value(pre_act).astype(jnp.bfloat16)
    mlp_rows = collect_rows(jnp.dot(act_rows, down_full, preferred_element_type=jnp.float32))
    result = (resid_rows + mlp_rows + biases_all[3]).astype(jnp.bfloat16)
    backward_set = (
        lax.all_gather(attention_in, "fsdp", axis=0, tiled=True),
        lax.all_gather(attention_out, "fsdp", axis=1, tiled=True),
        lax.all_gather(hidden_in, "fsdp", axis=0, tiled=True),
        lax.all_gather(hidden_out, "fsdp", axis=1, tiled=True),
        lax.all_gather(query_bias, "fsdp", axis=1, tiled=True),
        lax.all_gather(value_bias, "fsdp", axis=1, tiled=True),
        lax.all_gather(hidden_bias, "fsdp", axis=1, tiled=True),
    )
    in_back = backward_set[0]
    out_back = backward_set[1]
    up_back = backward_set[2]
    down_back = backward_set[3]
    grad_rows = output_grad.astype(jnp.float32)
    grad_all = spread_grads(output_grad)
    g_down = jnp.dot(act_rows.T, grad_all, preferred_element_type=jnp.float32)
    g_act = jnp.dot(grad_all, down_back.T, preferred_element_type=jnp.float32)
    g_pre = g_act * gelu_slope(pre_act)
    g_hidden_add = jnp.sum(g_pre, axis=0).reshape(hidden_add.shape)
    g_pre_b = g_pre.astype(jnp.bfloat16)
    g_up = jnp.dot(in_two.T, g_pre_b, preferred_element_type=jnp.float32)
    g_norm_two = collect_grads(jnp.dot(g_pre_b, up_back.T, preferred_element_type=jnp.float32))
    g_resid = grad_rows + normalize_back(g_norm_two, normed_two, inverse_two, gains_all[1])
    g_resid_all = spread_grads(g_resid.astype(jnp.bfloat16))
    g_out = jnp.dot(mixed_rows.T, g_resid_all, preferred_element_type=jnp.float32)
    g_mixed = (
        jnp.dot(g_resid_all, out_back.T, preferred_element_type=jnp.float32)
        .astype(jnp.bfloat16)
        .reshape(head_shape)
    )
    scores_again = head_scores(query_rows, key_rows, allowed, score_scale)
    probs = jnp.exp(scores_again - log_total)
    g_values = jnp.einsum(
        "shqk,sqhe->skhe", probs.astype(jnp.bfloat16), g_mixed, preferred_element_type=jnp.float32
    )
    g_probs = jnp.einsum("sqhe,skhe->shqk", g_mixed, value_rows, preferred_element_type=jnp.float32)
    inner_sum = jnp.sum(probs * g_probs, axis=-1, keepdims=True)
    g_scores = (probs * (g_probs - inner_sum) * score_scale).astype(jnp.bfloat16)
    g_query = jnp.einsum(
        "shqk,skhe->sqhe", g_scores, key_rows, preferred_element_type=jnp.float32
    ).reshape(-1, local_width)
    g_keys = jnp.einsum(
        "shqk,sqhe->skhe", g_scores, query_rows, preferred_element_type=jnp.float32
    ).reshape(-1, local_width)
    g_values = g_values.reshape(-1, local_width)
    g_query_add = jnp.sum(g_query, axis=0).reshape(query_add.shape)
    g_value_add = jnp.sum(g_values, axis=0).reshape(value_add.shape)
    g_proj = (
        jnp.stack([g_query, g_keys, g_values], axis=1)
        .astype(jnp.bfloat16)
        .reshape(-1, 3 * local_width)
    )
    g_in = jnp.dot(in_one.T, g_proj, preferred_element_type=jnp.float32).reshape(
        model_width, 3, local_width
    )
    g_norm_one = collect_grads(
        jnp.dot(
            g_proj,
            in_back.reshape(model_width, 3 * local_width).T,
            preferred_element_type=jnp.float32,
        )
    )
    tokens_grad = (
        g_resid + normalize_back(g_norm_one, normed_one, inverse_one, gains_all[0])
    ).astype(jnp.bfloat16)
    weight_sums = (
        lax.psum_scatter(g_in, "fsdp", scatter_dimension=0, tiled=True),
        lax.psum_scatter(g_out, "fsdp", scatter_dimension=1, tiled=True),
        lax.psum_scatter(g_up, "fsdp", scatter_dimension=0, tiled=True),
        lax.psum_scatter(g_down, "fsdp", scatter_dimension=1, tiled=True),
        lax.psum_scatter(g_query_add, "fsdp", scatter_dimension=1, tiled=True),
        lax.psum_scatter(g_value_add, "fsdp", scatter_dimension=1, tiled=True),
        lax.psum_scatter(g_hidden_add, "fsdp", scatter_dimension=1, tiled=True),
    )
    gain_terms = jnp.stack(
        [jnp.sum(g_norm_one * normed_one, axis=0), jnp.sum(g_norm_two * normed_two, axis=0)]
    )
    bias_terms = jnp.stack(
        [
            jnp.sum(g_norm_one, axis=0),
            jnp.sum(g_resid, axis=0),
            jnp.sum(g_norm_two, axis=0),
            jnp.sum(grad_rows, axis=0),
        ]
    )
    gains_grad, biases_grad = (
        lax.psum_scatter(gain_terms, ("fsdp", "tensor"), scatter_dimension=1, tiled=True),
        lax.psum_scatter(bias_terms, ("fsdp", "tensor"), scatter_dimension=1, tiled=True),
    )
    return (
        result,
        tokens_grad,
        weight_sums[0],
        weight_sums[1],
        weight_sums[2],
        weight_sums[3],
        weight_sums[4],
        weight_sums[5],
        weight_sums[6],
        gains_grad,
        biases_grad,
    )


def solution(mesh):
    placed = (
        P(("fsdp", "tensor"), None),
        P("fsdp", None),
        P(None, ("fsdp", "tensor")),
        P(None, ("fsdp", "tensor")),
        P("fsdp", None, "tensor"),
        P("tensor", "fsdp"),
        P("tensor", "fsdp"),
        P("tensor", "fsdp"),
        P("fsdp", "tensor"),
        P("tensor", "fsdp"),
        P("tensor", "fsdp"),
        P(("fsdp", "tensor"), None),
    )
    return jax.shard_map(
        shards,
        mesh=mesh,
        in_specs=placed,
        out_specs=(
            P(("fsdp", "tensor"), None),
            P(("fsdp", "tensor"), None),
            P("fsdp", None, "tensor"),
            P("tensor", "fsdp"),
            P("fsdp", "tensor"),
            P("tensor", "fsdp"),
            P("tensor", "fsdp"),
            P("tensor", "fsdp"),
            P("tensor", "fsdp"),
            P(None, ("fsdp", "tensor")),
            P(None, ("fsdp", "tensor")),
        ),
        check_vma=False,
    )
```

profile of v0, /device:TPU:0, one launch (start us, length us, event | category | flops | bytes accessed | tf_op | source)
XLA Modules:
  0.0 1231.3 jit_solution(13133017960299289246)
XLA Ops:
  8.0 70.2 %all-gather = f32[32,32,2]{1,2,0:T(2,128)S(1)} all-gather(f32[1,32,2]{1,2,0:T(2,128)} %bitcast.173), channel_id=1, replica_groups=mesh['fsdp'=16,'tensor'=2] {'fsdp','tensor'}, dimensions={0}, use_global_device_ids=true | all-gather | bytes 8448 | tf_op jit(solution)/shard_map/all_gather | solution.py:107
  78.3 63.9 %all-gather.1 = f32[32,32,4]{1,2,0:T(4,128)S(1)} all-gather(f32[1,32,4]{1,2,0:T(4,128)} %bitcast.171), channel_id=1, replica_groups=mesh['fsdp'=16,'tensor'=2] {'fsdp','tensor'}, dimensions={0}, use_global_device_ids=true | all-gather | bytes 16896 | tf_op jit(solution)/shard_map/all_gather | solution.py:108
  147.8 17.4 %all-gather.3 = bf16[16,4,8]{2,1,0:T(4,128)(2,1)S(1)} all-gather(bf16[1,4,8]{2,1,0:T(4,128)(2,1)} %bitcast.174), channel_id=1, replica_groups=mesh['fsdp'=16,'tensor'=2] {'fsdp'}, dimensions={0}, use_global_device_ids=true | all-gather | bytes 1088 | tf_op jit(solution)/shard_map/all_gather | solution.py:102
  165.3 19.2 %all-gather.2 = bf16[16,4,8]{2,1,0:T(4,128)(2,1)S(1)} all-gather(bf16[1,4,8]{2,1,0:T(4,128)(2,1)} %bitcast.175), channel_id=1, replica_groups=mesh['fsdp'=16,'tensor'=2] {'fsdp'}, dimensions={0}, use_global_device_ids=true | all-gather | bytes 1088 | tf_op jit(solution)/shard_map/all_gather | solution.py:103
  210.3 18.7 %reduce-scatter.18.cloned.1.call-done = bf16[256,1024]{1,0:T(8,128)(2,1)} async-done(((bf16[512,1024]{1,0:T(8,128)(2,1)}), bf16[256,1024]{1,0:T(8,128)(2,1)}) %reduce-scatter.18.cloned.1.call-update) | async-done | bytes 524304 | tf_op jit(solution)/shard_map/reduce_scatter | solution.py:68
  235.5 21.7 %all-gather.4 = bf16[16,16,8]{1,2,0:T(8,128)(2,1)S(1)} all-gather(bf16[1,16,8]{1,2,0:T(8,128)(2,1)S(1)} %bitcast.172), channel_id=1, replica_groups=mesh['fsdp'=16,'tensor'=2] {'fsdp'}, dimensions={0}, use_global_device_ids=true | all-gather | bytes 4352 | tf_op jit(solution)/shard_map/all_gather | solution.py:104
  257.3 24.7 %all-gather.22.cloned.1.call-done = bf16[1024,2048]{1,0:T(8,128)(2,1)} async-done(((bf16[64,2048]{1,0:T(8,128)(2,1)}), bf16[1024,2048]{1,0:T(8,128)(2,1)}) %all-gather.22.cloned.1.call-update) | async-done | bytes 4194320 | tf_op jit(solution)/shard_map/all_gather | solution.py:100
  282.0 21.9 %all-gather.20.cloned.1.call-done = bf16[512,1024]{1,0:T(8,128)(2,1)} async-done(((bf16[256,1024]{1,0:T(8,128)(2,1)}), bf16[512,1024]{1,0:T(8,128)(2,1)}) %all-gather.20.cloned.1.call-update) | async-done | bytes 1048592 | tf_op jit(solution)/shard_map/all_gather | solution.py:64
  310.7 16.1 %all-gather.26.cloned.1.call-done = bf16[512,1024]{1,0:T(8,128)(2,1)} async-done(((bf16[256,1024]{1,0:T(8,128)(2,1)}), bf16[512,1024]{1,0:T(8,128)(2,1)}) %all-gather.26.cloned.1.call-update) | async-done | bytes 1048592 | tf_op jit(solution)/shard_map/all_gather | solution.py:74
  326.8 53.1 %all-gather.24.cloned.1.call-done = bf16[2048,1024]{0,1:T(8,128)(2,1)} async-done(((bf16[2048,64]{0,1:T(8,128)(2,1)}), bf16[2048,1024]{0,1:T(8,128)(2,1)}) %all-gather.24.cloned.1.call-update) | async-done | bytes 4194320 | tf_op jit(solution)/shard_map/all_gather | solution.py:101
  400.6 11.5 reduce-scatter.22.cloned.1.call-done
  413.8 20.7 %reduce-scatter.20.cloned.1.call-done = bf16[256,1024]{1,0:T(8,128)(2,1)} async-done(((bf16[512,1024]{1,0:T(8,128)(2,1)}), bf16[256,1024]{1,0:T(8,128)(2,1)}) %reduce-scatter.20.cloned.1.call-update) | async-done | bytes 524304 | tf_op jit(solution)/shard_map/reduce_scatter | solution.py:68
  438.6 21.2 %all-gather.28.cloned.1.call-done = bf16[512,1024]{1,0:T(8,128)(2,1)} async-done(((bf16[256,1024]{1,0:T(8,128)(2,1)}), bf16[512,1024]{1,0:T(8,128)(2,1)}) %all-gather.28.cloned.1.call-update) | async-done | bytes 1048592 | tf_op jit(solution)/shard_map/all_gather | solution.py:74
  473.3 14.2 %fusion.8 = bf16[8,64,512]{2,1,0:T(8,128)(2,1)} fusion(f32[8,512,512]{1,2,0:T(8,128)} %fusion.75, f32[8,512,512]{1,2,0:T(8,128)} %copy-done.1, f32[8,512]{1,0:T(8,128)S(1)} %log_add_fusion, pred[512,512]{0,1:T(8,128)(4,1)S(1)} %fusion.73, f32[512,8,64]{0,2,1:T(8,128)S(1)} %bitcast.124, f32[8,64]{1,0:T(8,128)S(1)} %copy.52), kind=kOutput, calls=%fused_computation.13 | convolution fusion | flops 292033024 | bytes 18630656 | tf_op jit(solution)/shard_map/shqk,sqhe->skhe/dot_general | solution.py:194
  487.5 14.1 %bitcast_reduce_fusion.1 = (f32[8,64]{1,0:T(8,128)S(1)}, bf16[8,64,512]{2,1,0:T(8,128)(2,1)}) fusion(bf16[512,8,64]{0,2,1:T(8,128)(2,1)S(1)} %bitcast.128, f32[8,512,512]{1,2,0:T(8,128)} %fusion.75, f32[8,512,512]{1,2,0:T(8,128)} %copy-done.1, f32[8,512]{1,0:T(8,128)S(1)} %log_add_fusion, pred[512,512]{0,1:T(8,128)(4,1)S(1)} %fusion.73), kind=kOutput, calls=%fused_computation.81 | convolution fusion | flops 292032512 | bytes 18106368 | tf_op jit(solution)/shard_map/shqk,skhe->sqhe/dot_general | solution.py:191
  510.9 19.3 %reduce-scatter.24.cloned.1.call-done = bf16[256,1024]{1,0:T(8,128)(2,1)} async-done(((bf16[512,1024]{1,0:T(8,128)(2,1)}), bf16[256,1024]{1,0:T(8,128)(2,1)}) %reduce-scatter.24.cloned.1.call-update) | async-done | bytes 524304 | tf_op jit(solution)/shard_map/reduce_scatter | solution.py:78
  564.4 24.3 %reduce-scatter.34.cloned.1.call-done = f32[16,8]{1,0:T(8,128)} async-done(((f32[256,8]{1,0:T(8,128)}), f32[16,8]{1,0:T(8,128)}) %reduce-scatter.34.cloned.1.call-update) | async-done | bytes 528
  590.2 57.7 %all-reduce.2 = (f32[8,64]{0,1:T(8,128)S(1)}, f32[8,64]{0,1:T(8,128)S(1)}) all-reduce(f32[8,64]{0,1:T(8,128)S(1)} %copy.63, f32[8,64]{0,1:T(8,128)S(1)} %copy.64), channel_id=10, replica_groups=mesh['fsdp'=16,'tensor'=2] {'fsdp'}, use_global_device_ids=true, to_apply=%region_20.21.clone | all-reduce | flops 1024 | bytes 8192
  650.3 73.6 %reduce-scatter.36.cloned.1.call-done = f32[32,2]{1,0:T(8,128)} async-done(((f32[1024,2]{1,0:T(8,128)}), f32[32,2]{1,0:T(8,128)}) %reduce-scatter.36.cloned.1.call-update) | async-done | bytes 272
  725.2 130.5 %reduce-scatter.38.cloned.1.call-done = f32[32,4]{1,0:T(8,128)} async-done(((f32[1024,4]{1,0:T(8,128)}), f32[32,4]{1,0:T(8,128)}) %reduce-scatter.38.cloned.1.call-update) | async-done | bytes 528
  857.1 60.3 %reduce-scatter.28.cloned.1.call-done = f32[512,64]{0,1:T(8,128)} async-done(((f32[512,1024]{0,1:T(8,128)}), f32[512,64]{0,1:T(8,128)}) %reduce-scatter.28.cloned.1.call-update) | async-done | bytes 131088 | tf_op jit(solution)/shard_map/reduce_scatter | solution.py:220
  917.4 108.7 %reduce-scatter.32.cloned.1.call-done = f32[2048,64]{0,1:T(8,128)} async-done(((f32[2048,1024]{0,1:T(8,128)}), f32[2048,64]{0,1:T(8,128)}) %reduce-scatter.32.cloned.1.call-update) | async-done | bytes 524304 | tf_op jit(solution)/shard_map/reduce_scatter | solution.py:222
  1026.1 89.9 %reduce-scatter.26.cloned.1.call-done = f32[64,3,512]{2,0,1:T(8,128)} async-done(((f32[1024,3,512]{2,0,1:T(8,128)}), f32[64,3,512]{2,0,1:T(8,128)}) %reduce-scatter.26.cloned.1.call-update) | async-done | bytes 393232 | tf_op jit(solution)/shard_map/reduce_scatter | solution.py:219
  1116.0 108.4 %reduce-scatter.30.cloned.1.call-done = f32[64,2048]{1,0:T(8,128)} async-done(((f32[1024,2048]{1,0:T(8,128)}), f32[64,2048]{1,0:T(8,128)}) %reduce-scatter.30.cloned.1.call-update) | async-done | bytes 524304 | tf_op jit(solution)/shard_map/reduce_scatter | solution.py:221
  (153 shorter events, 134.4 us)
Async XLA Ops:
  7.2 178.5 %all-gather.16.cloned.1.call-start = ((), (), s32[]{:S(2)}) async-start(), calls=%async_computation.12 | async-start | bytes 3342336 | tf_op jit(solution)/shard_map/all_gather | solution.py:98
  7.9 182.4 %all-gather.14.cloned.1.call-start = ((), (), s32[]{:S(2)}) async-start(), calls=%async_computation.11 | async-start | bytes 1572864 | tf_op jit(solution)/shard_map/all_gather | solution.py:64
  147.0 59.6 %all-gather.18.cloned.1.call-start = ((), (), s32[]{:S(2)}) async-start(), calls=%async_computation.13 | async-start | bytes 1114112 | tf_op jit(solution)/shard_map/all_gather | solution.py:99
  147.8 81.3 %reduce-scatter.18.cloned.1.call-start = ((), (), s32[]{:S(2)}) async-start(), calls=%async_computation.14 | async-start | bytes 1572864 | tf_op jit(solution)/shard_map/reduce_scatter | solution.py:68
  202.3 31.6 %copy-start.12 = (bf16[8,64,512]{2,1,0:T(8,128)(2,1)}, bf16[8,64,512]{2,1,0:T(8,128)(2,1)S(1)}, u32[]{:S(2)}) copy-start(bf16[8,64,512]{2,1,0:T(8,128)(2,1)S(1)} %fusion.49) | copy-start | bytes 1572868
  202.3 26.7 %copy-start = (bf16[256,1024]{1,0:T(8,128)(2,1)S(1)}, bf16[256,1024]{1,0:T(8,128)(2,1)}, u32[]{:S(2)}) copy-start(bf16[256,1024]{1,0:T(8,128)(2,1)} %param.12) | copy-start | bytes 1572868
  206.6 28.8 %copy-start.15 = (bf16[8,16]{1,0:T(8,128)(2,1)S(1)}, bf16[8,16]{1,0:T(8,128)(2,1)}, u32[]{:S(2)}) copy-start(bf16[8,16]{1,0:T(8,128)(2,1)} %param.21) | copy-start | bytes 772
  209.7 72.3 %all-gather.22.cloned.1.call-start = ((), (), s32[]{:S(2)}) async-start(), calls=%async_computation.16 | async-start | bytes 4456448 | tf_op jit(solution)/shard_map/all_gather | solution.py:100
  210.3 93.6 %all-gather.20.cloned.1.call-start = ((), (), s32[]{:S(2)}) async-start(), calls=%async_computation.15 | async-start | bytes 1572864 | tf_op jit(solution)/shard_map/all_gather | solution.py:64
  233.9 92.9 %all-gather.26.cloned.1.call-start = ((), (), s32[]{:S(2)}) async-start(), calls=%async_computation.19 | async-start | bytes 1572864 | tf_op jit(solution)/shard_map/all_gather | solution.py:74
  234.7 145.3 %all-gather.24.cloned.1.call-start = ((), (), s32[]{:S(2)}) async-start(), calls=%async_computation.17 | async-start | bytes 4456448 | tf_op jit(solution)/shard_map/all_gather | solution.py:101
  235.4 176.6 %reduce-scatter.22.cloned.1.call-start = ((), (), s32[]{:S(2)}) async-start(), calls=%async_computation.20 | async-start | bytes 1572864 | tf_op jit(solution)/shard_map/reduce_scatter | solution.py:78
  393.1 41.4 %reduce-scatter.20.cloned.1.call-start = ((), (), s32[]{:S(2)}) async-start(), calls=%async_computation.18 | async-start | bytes 1572864 | tf_op jit(solution)/shard_map/reduce_scatter | solution.py:68
  400.5 59.2 %all-gather.28.cloned.1.call-start = ((), (), s32[]{:S(2)}) async-start(), calls=%async_computation.21 | async-start | bytes 1572864 | tf_op jit(solution)/shard_map/all_gather | solution.py:74
  438.3 91.9 %reduce-scatter.24.cloned.1.call-start = ((), (), s32[]{:S(2)}) async-start(), calls=%async_computation.22 | async-start | bytes 1572864 | tf_op jit(solution)/shard_map/reduce_scatter | solution.py:78
  509.6 24.4 %copy-start.11 = (bf16[512,1024]{1,0:T(8,128)(2,1)S(1)}, bf16[512,1024]{1,0:T(8,128)(2,1)}, u32[]{:S(2)}) copy-start(bf16[512,1024]{1,0:T(8,128)(2,1)} %all-gather.28.cloned.1.call-done) | copy-start | bytes 3145732
  509.7 79.0 %reduce-scatter.34.cloned.1.call-start = ((), (), s32[]{:S(2)}) async-start(), calls=%async_computation.27 | async-start | bytes 139264
  510.6 213.3 %reduce-scatter.36.cloned.1.call-start = ((), (), s32[]{:S(2)}) async-start(), calls=%async_computation.28 | async-start | bytes 540672
  532.9 322.9 %reduce-scatter.38.cloned.1.call-start = ((), (), s32[]{:S(2)}) async-start(), calls=%async_computation.29 | async-start | bytes 540672
  534.0 383.4 %reduce-scatter.28.cloned.1.call-start = ((), (), s32[]{:S(2)}) async-start(), calls=%async_computation.24 | async-start | bytes 2228224 | tf_op jit(solution)/shard_map/reduce_scatter | solution.py:220
  536.2 489.9 %reduce-scatter.32.cloned.1.call-start = ((), (), s32[]{:S(2)}) async-start(), calls=%async_computation.26 | async-start | bytes 8912896 | tf_op jit(solution)/shard_map/reduce_scatter | solution.py:222
  544.5 571.4 %reduce-scatter.26.cloned.1.call-start = ((), (), s32[]{:S(2)}) async-start(), calls=%async_computation.23 | async-start | bytes 6684672 | tf_op jit(solution)/shard_map/reduce_scatter | solution.py:219
  554.0 670.4 %reduce-scatter.30.cloned.1.call-start = ((), (), s32[]{:S(2)}) async-start(), calls=%async_computation.25 | async-start | bytes 8912896 | tf_op jit(solution)/shard_map/reduce_scatter | solution.py:221
  562.5 86.6 %copy-start.7 = (bf16[256,1024]{1,0:T(8,128)(2,1)S(1)}, bf16[256,1024]{1,0:T(8,128)(2,1)}, u32[]{:S(2)}) copy-start(bf16[256,1024]{1,0:T(8,128)(2,1)} %reduce-scatter.24.cloned.1.call-done) | copy-start | bytes 1572868
  (15 other events, 114.3 us)
Sparse Core Ops, SparseCore 0:
  10.2 48.2 all-gather.15
  147.1 19.2 all-gather.13
  168.6 37.9 all-gather.17
  209.8 19.1 reduce-scatter.17
  231.3 50.6 all-gather.21
  284.0 19.7 all-gather.19
  305.5 21.2 all-gather.25
  329.2 50.7 all-gather.23
  393.2 18.7 reduce-scatter.21
  414.2 20.3 reduce-scatter.19
  438.4 21.3 all-gather.27
  509.8 20.3 reduce-scatter.23
  533.6 55.0 reduce-scatter.33
  590.8 133.0 reduce-scatter.35
  726.1 129.6 reduce-scatter.37
  859.9 57.4 reduce-scatter.27
  922.5 103.5 reduce-scatter.31
  1031.0 84.9 reduce-scatter.25
  1120.6 103.7 reduce-scatter.29
where the time goes:
time: 1240 us; the launch traced here: 1230 us
  waiting for transfers between devices  811 us (65%)
  blocking collectives  250 us (20%)
  matrix products  108 us (9%)
  local copies, waits for them, and re-layouts  23.5 us (2%)
  other arithmetic  22 us (2%)
  between operations  15.5 us (1%)
    unnamed x22, waiting for transfers between devices  232 us
    reduce_scatter x1, waiting for transfers between devices, shards(): lax.psum_scatter(g_down, 'fsdp', scatter_dimension=1, tiled=True)  109 us
    reduce_scatter x1, waiting for transfers between devices, shards(): lax.psum_scatter(g_up, 'fsdp', scatter_dimension=0, tiled=True)  108 us
    reduce_scatter x1, waiting for transfers between devices, shards(): lax.psum_scatter(g_in, 'fsdp', scatter_dimension=0, tiled=True)  89.9 us
    all_gather x1, blocking collectives, shards(): lax.all_gather(norm_gains, ('fsdp', 'tensor'), axis=1, tiled=True)  70.2 us
    all_gather x1, blocking collectives, shards(): lax.all_gather(row_biases, ('fsdp', 'tensor'), axis=1, tiled=True)  63.9 us
    reduce_scatter x1, waiting for transfers between devices, shards(): lax.psum_scatter(g_out, 'fsdp', scatter_dimension=1, tiled=True)  60.3 us
    unnamed x1, blocking collectives  57.7 us
  transfers between devices with their start and end apart: 19, of which 17 were waited for; matrix products, arithmetic and copies ran while one was open for 7% of the time, Pallas kernels for 0%

commit v1 on v0

v1 whole, which is shorter than its diff:
```python
import math

import jax
import jax.numpy as jnp
from jax import lax
from jax.sharding import PartitionSpec as P

HD = 64
EPS = 1e-05
GELU_C = math.sqrt(2.0 / math.pi)
GELU_A = 0.044715
MASKED = -1e30
BF16 = jnp.bfloat16
F32 = jnp.float32


def gelu_parts(pre_act):
    square = pre_act * pre_act
    tanh_part = jnp.tanh(GELU_C * pre_act * (1.0 + GELU_A * square))
    half = 0.5 * (1.0 + tanh_part)
    slope = half + 0.5 * pre_act * (1.0 - tanh_part * tanh_part) * GELU_C * (
        1.0 + 3.0 * GELU_A * square
    )
    return pre_act * half, slope


def normalize(row_data):
    row_mean = jnp.mean(row_data, axis=-1, keepdims=True)
    centered = row_data - row_mean
    variance = jnp.mean(centered * centered, axis=-1, keepdims=True)
    inverse = lax.rsqrt(variance + EPS)
    return centered * inverse, inverse


def normalize_back(grad_rows, normed, inverse, gain_row):
    scaled = grad_rows * gain_row
    return inverse * (
        scaled
        - jnp.mean(scaled, axis=-1, keepdims=True)
        - normed * jnp.mean(scaled * normed, axis=-1, keepdims=True)
    )


def pair_mask(segments):
    places = jnp.arange(segments.shape[1])
    causal = places[:, None] >= places[None, :]
    same_doc = segments[:, :, None] == segments[:, None, :]
    return (causal[None] & same_doc)[:, None]


def head_scores(query_rows, key_rows, allowed, score_scale):
    scores = (
        jnp.einsum("sqhe,skhe->shqk", query_rows, key_rows, preferred_element_type=F32)
        * score_scale
    )
    return jnp.where(allowed, scores, MASKED)


def attend(query_rows, key_rows, value_rows, allowed, score_scale):
    scores = head_scores(query_rows, key_rows, allowed, score_scale)
    row_top = jnp.max(scores, axis=-1, keepdims=True)
    exp_terms = jnp.exp(scores - row_top)
    exp_total = jnp.sum(exp_terms, axis=-1, keepdims=True)
    log_total = row_top + jnp.log(exp_total)
    probs_b = (exp_terms / exp_total).astype(BF16)
    mixed = jnp.einsum("shqk,skhe->sqhe", probs_b, value_rows, preferred_element_type=F32)
    return mixed, log_total


def attend_back(query_rows, key_rows, value_rows, allowed, score_scale, log_total, g_mixed):
    scores_again = head_scores(query_rows, key_rows, allowed, score_scale)
    probs = jnp.exp(scores_again - log_total)
    g_values = jnp.einsum(
        "shqk,sqhe->skhe", probs.astype(BF16), g_mixed, preferred_element_type=F32
    )
    g_probs = jnp.einsum("sqhe,skhe->shqk", g_mixed, value_rows, preferred_element_type=F32)
    inner_sum = jnp.sum(probs * g_probs, axis=-1, keepdims=True)
    g_scores = (probs * (g_probs - inner_sum) * score_scale).astype(BF16)
    g_query = jnp.einsum("shqk,skhe->sqhe", g_scores, key_rows, preferred_element_type=F32)
    g_keys = jnp.einsum("shqk,sqhe->skhe", g_scores, query_rows, preferred_element_type=F32)
    return g_query, g_keys, g_values


def dot(left, right, dims):
    return lax.dot_general(left, right, (dims, ((), ())), preferred_element_type=F32)


class Ring:
    def __init__(self, n_fsdp):
        self.size = n_fsdp
        self.cores = 2
        self.second = n_fsdp // 8
        self.first = n_fsdp // (self.second * self.cores)

    def split(self, index):
        return (
            index // (self.second * self.cores),
            (index // self.cores) % self.second,
            index % self.cores,
        )

    def hop(self, value, first=0, second=0, core=0):
        pairs = []
        for source in range(self.size):
            a, b, c = self.split(source)
            a, b, c = (a + first) % self.first, (b + second) % self.second, (c + core) % self.cores
            pairs.append((source, (a * self.second + b) * self.cores + c))
        return lax.ppermute(value, "fsdp", pairs)

    def local_block(self, block):
        a, b, c = self.split(lax.axis_index("fsdp"))
        ga, gb, gc = self.split(block)
        r = (a - ga + self.first) % self.first
        xx = (b - gb + self.second) % self.second
        cc = (c - gc + self.cores) % self.cores
        return (cc * self.second + xx) * self.first + r

    def gather(self, block):
        current = [block]
        for _ in range(self.first - 1):
            current.append(self.hop(current[-1], first=1))
        own = list(current)
        for _ in range(self.second - 1):
            current = [self.hop(piece, second=1) for piece in current]
            own += current
        own = jnp.concatenate(own, axis=0)
        return jnp.concatenate([own, self.hop(own, core=1)], axis=0)

    def gather_small(self, block):
        own = [block] + [self.hop(block, first=r) for r in range(1, self.first)]
        current = own = jnp.concatenate(own, axis=0)
        for _ in range(self.second - 1):
            current = self.hop(current, second=1)
            own = jnp.concatenate([own, current], axis=0)
        return jnp.concatenate([own, self.hop(own, core=1)], axis=0)

    def scatter(self, blocks, link):
        half = blocks.shape[0] // self.cores
        total = blocks[:half] + self.hop(blocks[half:].astype(link), core=-1).astype(F32)
        quarter = half // self.second
        m = quarter // self.first
        acc = None
        for r in reversed(range(self.first)):
            piece = None
            for xx in reversed(range(self.second)):
                part = total[xx * quarter + r * m : xx * quarter + (r + 1) * m]
                if piece is not None:
                    part = part + self.hop(piece.astype(link), second=-1).astype(F32)
                piece = part
            if acc is not None:
                piece = piece + self.hop(acc.astype(link), first=-1).astype(F32)
            acc = piece
        return acc

    def scatter_small(self, blocks):
        half = blocks.shape[0] // self.cores
        total = blocks[:half] + self.hop(blocks[half:], core=-1)
        quarter = half // self.second
        acc = total[half - quarter :]
        for xx in reversed(range(self.second - 1)):
            acc = total[xx * quarter : (xx + 1) * quarter] + self.hop(acc, second=-1)
        m = quarter // self.first
        result = acc[:m]
        for r in range(1, self.first):
            result = result + self.hop(acc[r * m : (r + 1) * m], first=-r)
        return result


class Pair:
    def __init__(self, n_tensor):
        self.size = n_tensor

    def swap(self, value):
        return lax.ppermute(value, "tensor", [(0, 1), (1, 0)])

    def spread(self, own):
        if self.size != 2:
            return lax.all_gather(own, "tensor", axis=0, tiled=True)
        other = self.swap(own)
        first = lax.axis_index("tensor") == 0
        return jnp.concatenate(
            [jnp.where(first, own, other), jnp.where(first, other, own)], axis=0
        )

    def total(self, partial_rows):
        rounded = partial_rows.astype(BF16)
        if self.size != 2:
            return lax.psum(rounded.astype(F32), "tensor")
        return rounded.astype(F32) + self.swap(rounded).astype(F32)

    def collect(self, partial_rows):
        rounded = partial_rows.astype(BF16)
        if self.size != 2:
            return lax.psum_scatter(rounded, "tensor", scatter_dimension=0, tiled=True).astype(F32)
        rows = rounded.shape[0] // 2
        index = lax.axis_index("tensor")
        away = lax.dynamic_slice_in_dim(rounded, (1 - index) * rows, rows, 0)
        stay = lax.dynamic_slice_in_dim(rounded, index * rows, rows, 0)
        return stay.astype(F32) + self.swap(away).astype(F32)

    def collect_small(self, terms):
        if self.size != 2:
            return lax.psum_scatter(terms, "tensor", scatter_dimension=0, tiled=True)[0]
        index = lax.axis_index("tensor")
        return terms[index] + self.swap(terms[1 - index])

    def own(self, rows_all):
        rows = rows_all.shape[0] // self.size
        return lax.dynamic_slice_in_dim(rows_all, lax.axis_index("tensor") * rows, rows, 0)


def layer(n_fsdp, n_tensor):
    ring = Ring(n_fsdp)
    pair = Pair(n_tensor)

    def shards(
        tokens,
        segments,
        norm_gains,
        row_biases,
        attention_in,
        query_bias,
        value_bias,
        attention_out,
        hidden_in,
        hidden_bias,
        hidden_out,
        output_grad,
    ):
        m = attention_in.shape[0]
        model_width = m * n_fsdp
        local_width = attention_in.shape[2]
        heads = query_bias.shape[0]
        hidden_width = hidden_in.shape[1]
        seq_count, seq_len = segments.shape
        head_shape = (seq_count, seq_len, heads, HD)
        score_scale = 1.0 / math.sqrt(HD)
        q_len, h_len = query_bias.size, hidden_bias.size

        in_full = ring.gather(attention_in.reshape(m, 3 * local_width))
        out_t = ring.gather(attention_out.T)
        up_full = ring.gather(hidden_in)
        down_t = ring.gather(hidden_out.T)

        rows_six = jnp.concatenate([norm_gains, row_biases], axis=0)
        six_all = pair.spread(rows_six[None])
        six_all = six_all.transpose(1, 0, 2).reshape(1, 6 * m)
        flat = jnp.concatenate(
            [
                six_all,
                query_bias.astype(F32).reshape(1, q_len),
                value_bias.astype(F32).reshape(1, q_len),
                hidden_bias.astype(F32).reshape(1, h_len),
            ],
            axis=1,
        )
        small = ring.gather_small(flat)
        six_full = (
            small[:, : 6 * m].reshape(n_fsdp, 6, m).transpose(1, 0, 2).reshape(6, model_width)
        )
        gains_all, biases_all = six_full[:2], six_full[2:]
        block_ids = ring.local_block(jnp.arange(n_fsdp))
        to_global = (block_ids[:, None] == jnp.arange(n_fsdp)[None, :]).astype(BF16)
        head_small = dot(to_global, small[:, 6 * m :].astype(BF16), ((1,), (0,)))

        def head_row(start, length, width):
            return (
                head_small[:, start : start + length]
                .reshape(n_fsdp, heads, length // heads)
                .transpose(1, 0, 2)
                .reshape(width)
            )

        query_add = head_row(0, q_len, local_width)
        value_add = head_row(q_len, q_len, local_width)
        hidden_add = head_row(2 * q_len, h_len, hidden_width)

        places = jnp.arange(model_width)
        local_places = ring.local_block(places // m) * m + places % m
        to_local = (local_places[:, None] == places[None, :]).astype(BF16)
        tok_b = dot(pair.spread(tokens), to_local, ((1,), (0,))).astype(BF16)
        grad_all = dot(pair.spread(output_grad), to_local, ((1,), (0,))).astype(BF16)
        tok_rows = tok_b.astype(F32)
        grad_rows = grad_all.astype(F32)

        allowed = pair_mask(segments)
        normed_one, inverse_one = normalize(tok_rows)
        in_one = (normed_one * gains_all[0] + biases_all[0]).astype(BF16)
        projected = dot(in_one, in_full, ((1,), (0,)))
        query_rows = (projected[:, :local_width] + query_add).astype(BF16).reshape(head_shape)
        key_rows = projected[:, local_width : 2 * local_width].astype(BF16).reshape(head_shape)
        value_rows = (projected[:, 2 * local_width :] + value_add).astype(BF16).reshape(head_shape)
        mixed, log_total = attend(query_rows, key_rows, value_rows, allowed, score_scale)
        mixed_rows = mixed.reshape(-1, local_width).astype(BF16)
        attn_rows = pair.total(dot(mixed_rows, out_t, ((1,), (1,))))
        resid_rows = tok_rows + attn_rows + biases_all[1]
        normed_two, inverse_two = normalize(resid_rows)
        in_two = (normed_two * gains_all[1] + biases_all[2]).astype(BF16)
        pre_act = dot(in_two, up_full, ((1,), (0,))) + hidden_add
        act, slope = gelu_parts(pre_act)
        act_rows = act.astype(BF16)

        g_pre = dot(grad_all, down_t, ((1,), (0,))) * slope
        g_hidden_add = jnp.sum(g_pre, axis=0)
        g_pre_b = g_pre.astype(BF16)
        g_two_part = dot(g_pre_b, up_full, ((1,), (1,)))
        g_norm_two = pair.total(g_two_part)
        g_down_t = ring.scatter(dot(grad_all, act_rows, ((0,), (0,))), BF16)
        g_up = ring.scatter(dot(in_two, g_pre_b, ((0,), (0,))), BF16)

        mlp_rows = pair.collect(dot(act_rows, down_t, ((1,), (1,))))
        result = (pair.own(resid_rows) + mlp_rows + biases_all[3]).astype(BF16)
        result = dot(result, to_local, ((1,), (1,))).astype(BF16)

        g_resid = grad_rows + normalize_back(g_norm_two, normed_two, inverse_two, gains_all[1])
        g_resid_b = g_resid.astype(BF16)
        g_out_t = ring.scatter(dot(g_resid_b, mixed_rows, ((0,), (0,))), BF16)
        g_mixed = dot(g_resid_b, out_t, ((1,), (0,))).astype(BF16).reshape(head_shape)
        g_query, g_keys, g_values = attend_back(
            query_rows, key_rows, value_rows, allowed, score_scale, log_total, g_mixed
        )
        g_query = g_query.reshape(-1, local_width)
        g_keys = g_keys.reshape(-1, local_width)
        g_values = g_values.reshape(-1, local_width)
        g_query_add = jnp.sum(g_query, axis=0)
        g_value_add = jnp.sum(g_values, axis=0)
        g_proj = jnp.concatenate([g_query, g_keys, g_values], axis=1).astype(BF16)
        g_in = ring.scatter(dot(in_one, g_proj, ((0,), (0,))), BF16)
        g_one_part = dot(g_proj, in_full, ((1,), (1,)))
        g_norm_one = pair.collect(g_one_part)
        tokens_grad = (
            pair.own(g_resid)
            + normalize_back(g_norm_one, pair.own(normed_one), pair.own(inverse_one), gains_all[0])
        ).astype(BF16)
        tokens_grad = dot(tokens_grad, to_local, ((1,), (1,))).astype(BF16)

        own_grad = pair.own(grad_rows)
        six_terms = jnp.stack(
            [
                jnp.sum(g_one_part * normed_one, axis=0),
                jnp.sum(g_two_part * normed_two, axis=0),
                jnp.sum(g_one_part, axis=0),
                jnp.sum(pair.own(g_resid), axis=0),
                jnp.sum(g_two_part, axis=0),
                jnp.sum(own_grad, axis=0),
            ]
        )
        six_terms = six_terms.reshape(6, n_fsdp, m).transpose(1, 0, 2).reshape(n_fsdp, 6 * m)

        def head_blocks(row, length):
            return (
                row.reshape(heads, n_fsdp, length // heads)
                .transpose(1, 0, 2)
                .reshape(n_fsdp, length)
            )

        head_terms = jnp.concatenate(
            [
                head_blocks(g_query_add, q_len),
                head_blocks(g_value_add, q_len),
                head_blocks(g_hidden_add, h_len),
            ],
            axis=1,
        )
        head_terms = lax.dot_general(
            to_global.astype(F32),
            head_terms,
            (((0,), (0,)), ((), ())),
            precision=lax.Precision.HIGHEST,
            preferred_element_type=F32,
        )
        sums = ring.scatter_small(jnp.concatenate([six_terms, head_terms], axis=1))[0]
        six_sum = sums[: 6 * m].reshape(6, n_tensor, m // n_tensor).transpose(1, 0, 2)
        six_sum = pair.collect_small(six_sum)
        head_sum = sums[6 * m :]
        return (
            result,
            tokens_grad,
            g_in.reshape(m, 3, local_width),
            g_out_t.T,
            g_up,
            g_down_t.T,
            head_sum[:q_len].reshape(query_bias.shape),
            head_sum[q_len : 2 * q_len].reshape(value_bias.shape),
            head_sum[2 * q_len :].reshape(hidden_bias.shape),
            six_sum[:2],
            six_sum[2:],
        )

    return shards


def solution(mesh):
    n_fsdp = mesh.shape["fsdp"]
    n_tensor = mesh.shape["tensor"]
    rows = P(("fsdp", "tensor"), None)
    columns = P(None, ("fsdp", "tensor"))
    head = P("tensor", "fsdp")
    into = P("fsdp", None, "tensor")
    up = P("fsdp", "tensor")
    return jax.shard_map(
        layer(n_fsdp, n_tensor),
        mesh=mesh,
        in_specs=(
            rows,
            P("fsdp", None),
            columns,
            columns,
            into,
            head,
            head,
            head,
            up,
            head,
            head,
            rows,
        ),
        out_specs=(rows, rows, into, head, up, head, head, head, head, columns, columns),
        check_vma=False,
    )
```

time: 1240 us -> 479 us (0.39)
  waiting for transfers between devices: 811 us -> 199 us
  blocking collectives: 250 us -> 0 us
  starting transfers between devices: 1.24 us -> 99 us
  local copies, waits for them, and re-layouts: 23.5 us -> 60 us
  matrix products: 108 us -> 84.9 us
  between operations: 15.5 us -> 2.34 us
    reduce_scatter x8 -> x0, waiting for transfers between devices: 437 us -> none  [the longest x1 109 us: shards(): lax.psum_scatter(g_down, 'fsdp', scatter_dimension=1, tiled=True)]
    unnamed x22 -> x0, waiting for transfers between devices: 232 us -> none
    ppermute x0 -> x82, waiting for transfers between devices: none -> 199 us  [the longest x74 151 us: hop(): return lax.ppermute(value, 'fsdp', pairs)]
    all_gather x5 -> x0, blocking collectives: 193 us -> none  [the longest x1 70.2 us: shards(): lax.all_gather(norm_gains, ('fsdp', 'tensor'), axis=1, tiled=True)]
    all_gather x8 -> x0, waiting for transfers between devices: 141 us -> none  [the longest x1 53.1 us: shards(): lax.all_gather(hidden_out, 'fsdp', axis=1, tiled=True)]
    ppermute x0 -> x82, starting transfers between devices: none -> 99 us  [the longest x74 90.8 us: hop(): return lax.ppermute(value, 'fsdp', pairs)]
    unnamed x1 -> x0, blocking collectives: 57.7 us -> none
    dot_general x17 -> x23, matrix products: 107 us -> 83.4 us  [the longest x17 43.7 us: dot(): lax.dot_general(left, right, (dims, ((), ())), preferred_element_type=F32)]
  transfers between devices with their start and end apart: 19 -> 82, of which waited for: 17 -> 41; matrix products, arithmetic and copies ran while one was open for 7% -> 31% of each run, Pallas kernels for 0% -> 0%
where the time goes in v1:
time: 479 us; the launch traced here: 473 us
  waiting for transfers between devices  199 us (42%)
  starting transfers between devices  99 us (21%)
  matrix products  84.9 us (18%)
  local copies, waits for them, and re-layouts  60 us (13%)
  other arithmetic  28 us (6%)
    ppermute x74, waiting for transfers between devices, hop(): return lax.ppermute(value, 'fsdp', pairs)  151 us
    ppermute x74, starting transfers between devices, hop(): return lax.ppermute(value, 'fsdp', pairs)  90.8 us
    ppermute x8, waiting for transfers between devices, swap(): return lax.ppermute(value, 'tensor', [(0, 1), (1, 0)])  47.1 us
    dot_general x17, matrix products, dot(): lax.dot_general(left, right, (dims, ((), ())), preferred_element_type=F32)  43.7 us
    unnamed x151, local copies, waits for them, and re-layouts  32.6 us
    dot_general x1, matrix products, attend_back(): jnp.einsum('shqk,skhe->sqhe', g_scores, key_rows, preferred_element_type=...  14.5 us
    dot_general x1, matrix products, attend_back(): jnp.einsum('shqk,sqhe->skhe', g_scores, query_rows, preferred_element_typ...  14.2 us
  transfers between devices with their start and end apart: 82, of which 41 were waited for; matrix products, arithmetic and copies ran while one was open for 31% of the time, Pallas kernels for 0%

profile of v1, /device:TPU:0, one launch (start us, length us, event | category | flops | bytes accessed | tf_op | source)
XLA Modules:
  0.0 472.8 jit_solution(11933485841444853369)
XLA Ops:
  38.8 5.4 %collective-permute-done.16 = bf16[64,512]{1,0:T(8,128)(2,1)S(1)} collective-permute-done((bf16[64,512]{1,0:T(8,128)(2,1)S(1)}, bf16[64,512]{1,0:T(8,128)(2,1)S(1)}, u32[]{:S(2)}, u32[]{:S(2)}) %collective-permute-start.16) | collective-permute-done | bytes 65568 | tf_op jit(solution)/shard_map/ppermute | solution.py:108
  44.9 5.4 %collective-permute-done.17 = bf16[64,512]{1,0:T(8,128)(2,1)S(1)} collective-permute-done((bf16[64,512]{1,0:T(8,128)(2,1)S(1)}, bf16[64,512]{1,0:T(8,128)(2,1)S(1)}, u32[]{:S(2)}, u32[]{:S(2)}) %collective-permute-start.17) | collective-permute-done | bytes 65568 | tf_op jit(solution)/shard_map/ppermute | solution.py:108
  74.5 7.8 %collective-permute-done.8 = bf16[64,1536]{1,0:T(8,128)(2,1)S(1)} collective-permute-done((bf16[64,1536]{1,0:T(8,128)(2,1)S(1)}, bf16[64,1536]{1,0:T(8,128)(2,1)S(1)}, u32[]{:S(2)}, u32[]{:S(2)}) %collective-permute-start.8) | collective-permute-done | bytes 196640 | tf_op jit(solution)/shard_map/ppermute | solution.py:108
  88.5 5.0 %collective-permute-done.33 = bf16[64,2048]{1,0:T(8,128)(2,1)S(1)} collective-permute-done((bf16[64,2048]{1,0:T(8,128)(2,1)}, bf16[64,2048]{1,0:T(8,128)(2,1)S(1)}, u32[]{:S(2)}, u32[]{:S(2)}) %collective-permute-start.33) | collective-permute-done | bytes 262176 | tf_op jit(solution)/shard_map/ppermute | solution.py:108
  97.1 6.6 %collective-permute-done.9 = bf16[64,1536]{1,0:T(8,128)(2,1)S(1)} collective-permute-done((bf16[64,1536]{1,0:T(8,128)(2,1)S(1)}, bf16[64,1536]{1,0:T(8,128)(2,1)S(1)}, u32[]{:S(2)}, u32[]{:S(2)}) %collective-permute-start.9) | collective-permute-done | bytes 196640 | tf_op jit(solution)/shard_map/ppermute | solution.py:108
  105.4 5.8 %collective-permute-done.12 = bf16[64,1536]{1,0:T(8,128)(2,1)S(1)} collective-permute-done((bf16[64,1536]{1,0:T(8,128)(2,1)S(1)}, bf16[64,1536]{1,0:T(8,128)(2,1)S(1)}, u32[]{:S(2)}, u32[]{:S(2)}) %collective-permute-start.12) | collective-permute-done | bytes 196640 | tf_op jit(solution)/shard_map/ppermute | solution.py:108
  122.8 11.9 %collective-permute-done.13 = bf16[64,1536]{1,0:T(8,128)(2,1)S(1)} collective-permute-done((bf16[64,1536]{1,0:T(8,128)(2,1)S(1)}, bf16[64,1536]{1,0:T(8,128)(2,1)S(1)}, u32[]{:S(2)}, u32[]{:S(2)}) %collective-permute-start.13) | collective-permute-done | bytes 196640 | tf_op jit(solution)/shard_map/ppermute | solution.py:108
  135.9 7.8 %collective-permute-done.26 = bf16[64,2048]{1,0:T(8,128)(2,1)S(1)} collective-permute-done((bf16[64,2048]{1,0:T(8,128)(2,1)S(1)}, bf16[64,2048]{1,0:T(8,128)(2,1)S(1)}, u32[]{:S(2)}, u32[]{:S(2)}) %collective-permute-start.26) | collective-permute-done | bytes 262176 | tf_op jit(solution)/shard_map/ppermute | solution.py:108
  154.0 4.3 collective-permute-done.38
  183.8 15.7 %collective-permute-done.23 = bf16[512,1024]{1,0:T(8,128)(2,1)} collective-permute-done((bf16[512,1024]{1,0:T(8,128)(2,1)S(1)}, bf16[512,1024]{1,0:T(8,128)(2,1)}, u32[]{:S(2)}, u32[]{:S(2)}) %collective-permute-start.23) | collective-permute-done | bytes 1048608 | tf_op jit(solution)/shard_map/ppermute | solution.py:174
  206.9 4.7 %fusion.207 = (f32[2048]{0:T(1024)S(1)}, bf16[512,2048]{1,0:T(8,128)(2,1)S(1)}) fusion(f32[512,2048]{1,0:T(8,128)S(1)} %fusion.185, f32[2048]{0:T(1024)S(1)} %add.519, bf16[512,1024]{1,0:T(8,128)(2,1)S(1)} %copy-done.17, bf16[1024,2048]{1,0:T(8,128)(2,1)S(1)} %copy-done.38), kind=kOutput, calls=%fused_computation.393 | convolution fusion | flops 2168453120 | bytes 11550720 | tf_op jit(solution)/shard_map/dot_general | solution.py:85
  231.6 23.1 %collective-permute-done.40 = bf16[256,1024]{1,0:T(8,128)(2,1)} collective-permute-done((bf16[256,1024]{1,0:T(8,128)(2,1)}, bf16[256,1024]{1,0:T(8,128)(2,1)}, u32[]{:S(2)}, u32[]{:S(2)}) %collective-permute-start.40) | collective-permute-done | bytes 524320 | tf_op jit(solution)/shard_map/ppermute | solution.py:174
  265.5 4.8 %fusion.209 = f32[8,512,512]{1,2,0:T(8,128)} fusion(bf16[512,8,64]{0,2,1:T(8,128)(2,1)S(1)} %bitcast.102, bf16[512,8,64]{0,2,1:T(8,128)(2,1)S(1)} %bitcast.109), kind=kOutput, calls=%fused_computation.395 | convolution fusion | flops 268435456 | bytes 9437184 | tf_op jit(solution)/shard_map/sqhe,skhe->shqk/dot_general | solution.py:76
  273.4 14.2 %fusion.57 = bf16[8,64,512]{2,1,0:T(8,128)(2,1)} fusion(bf16[512,8,64]{0,2,1:T(8,128)(2,1)S(1)} %bitcast.107, f32[8,512,512]{1,2,0:T(8,128)} %fusion.209, f32[8,512,512]{1,2,0:T(8,128)} %copy-done, f32[8,512]{1,0:T(8,128)S(1)} %copy-done.39, pred[512,512]{0,1:T(8,128)(4,1)S(1)} %fusion.72), kind=kOutput, calls=%fused_computation.70 | convolution fusion | flops 291770880 | bytes 18104320 | tf_op jit(solution)/shard_map/shqk,sqhe->skhe/dot_general | solution.py:80
  287.6 14.5 %fusion.199 = (f32[8,64]{1,0:T(8,128)S(1)}, bf16[1,512,8,64]{1,3,2,0:T(8,128)(2,1)}) fusion(bf16[512,8,64]{0,2,1:T(8,128)(2,1)} %bitcast.105, f32[8,512,512]{1,2,0:T(8,128)} %fusion.209, f32[8,512,512]{1,2,0:T(8,128)} %copy-done, f32[8,512]{1,0:T(8,128)S(1)} %copy-done.39, pred[512,512]{0,1:T(8,128)(4,1)S(1)} %fusion.72), kind=kOutput, calls=%fused_computation.387 | convolution fusion | flops 292032512 | bytes 18106368 | tf_op jit(solution)/shard_map/shqk,skhe->sqhe/dot_general | solution.py:79
  302.7 6.2 %fusion.189 = (f32[1024]{0:T(1024)S(1)}, f32[1024]{0:T(1024)S(1)}, bf16[512,1024]{1,0:T(8,128)(2,1)}, f32[512,1024]{1,0:T(8,128)}) fusion(f32[512]{0:T(512)S(1)} %copy-done.46, f32[512]{0:T(512)S(1)} %copy-done.43, bf16[512,1024]{1,0:T(8,128)(2,1)S(1)} %get-tuple-element.183, bf16[1024,1536]{1,0:T(8,128)(2,1)} %copy-done.41, ...), kind=kOutput, calls=%fused_computation.378 | convolution fusion | flops 1618999296 | bytes 8925184 | tf_op jit(solution)/shard_map/dot_general | solution.py:85
  328.7 8.3 %collective-permute-done.81 = f32[6,32]{1,0:T(8,128)S(1)} collective-permute-done((f32[6,32]{1,0:T(8,128)S(1)}, f32[6,32]{1,0:T(8,128)S(1)}, u32[]{:S(2)}, u32[]{:S(2)}) %collective-permute-start.81) | collective-permute-done | bytes 800 | tf_op jit(solution)/shard_map/ppermute | solution.py:174
  376.6 18.2 %collective-permute-done.72 = bf16[64,2048]{1,0:T(8,128)(2,1)S(1)} collective-permute-done((bf16[64,2048]{1,0:T(8,128)(2,1)S(1)}, bf16[64,2048]{1,0:T(8,128)(2,1)S(1)}, u32[]{:S(2)}, u32[]{:S(2)}) %collective-permute-start.72) | collective-permute-done | bytes 262176 | tf_op jit(solution)/shard_map/ppermute | solution.py:108
  413.9 5.5 %collective-permute-done.48 = bf16[64,1536]{1,0:T(8,128)(2,1)S(1)} collective-permute-done((bf16[64,1536]{1,0:T(8,128)(2,1)S(1)}, bf16[64,1536]{1,0:T(8,128)(2,1)S(1)}, u32[]{:S(2)}, u32[]{:S(2)}) %collective-permute-start.48) | collective-permute-done | bytes 196640 | tf_op jit(solution)/shard_map/ppermute | solution.py:108
  419.4 4.9 %collective-permute-start.66 = (bf16[64,2048]{1,0:T(8,128)(2,1)S(1)}, bf16[64,2048]{1,0:T(8,128)(2,1)S(1)}, u32[]{:S(2)}, u32[]{:S(2)}) collective-permute-start(bf16[64,2048]{1,0:T(8,128)(2,1)S(1)} %fusion.85), channel_id=1, source_target_pairs={{0,24},{2,26},{4,28},{6,30},{8,0},{10,2},{12,4},{14,6},{16,8},{18,... | collective-permute-start | bytes 786440 | tf_op jit(solution)/shard_map/ppermute | solution.py:108
  424.6 5.1 %collective-permute-done.66 = bf16[64,2048]{1,0:T(8,128)(2,1)S(1)} collective-permute-done((bf16[64,2048]{1,0:T(8,128)(2,1)S(1)}, bf16[64,2048]{1,0:T(8,128)(2,1)S(1)}, u32[]{:S(2)}, u32[]{:S(2)}) %collective-permute-start.66) | collective-permute-done | bytes 262176 | tf_op jit(solution)/shard_map/ppermute | solution.py:108
  429.8 4.3 collective-permute-start.74
  434.2 6.5 %collective-permute-done.74 = bf16[64,2048]{1,0:T(8,128)(2,1)S(1)} collective-permute-done((bf16[64,2048]{1,0:T(8,128)(2,1)S(1)}, bf16[64,2048]{1,0:T(8,128)(2,1)S(1)}, u32[]{:S(2)}, u32[]{:S(2)}) %collective-permute-start.74) | collective-permute-done | bytes 262176 | tf_op jit(solution)/shard_map/ppermute | solution.py:108
  464.0 4.3 collective-permute-start.51
  (454 shorter events, 270.1 us)
Async XLA Ops:
  0.7 65.1 %collective-permute-start.32 = (bf16[64,2048]{1,0:T(8,128)(2,1)}, bf16[64,2048]{1,0:T(8,128)(2,1)}, u32[]{:S(2)}, u32[]{:S(2)}) collective-permute-start(bf16[64,2048]{1,0:T(8,128)(2,1)} %bitcast.117), channel_id=1, source_target_pairs={{0,8},{2,10},{4,12},{6,14},{8,16},{10,18},{12,20},{14,22},{16,24},... | collective-permute-start | bytes 786440 | tf_op jit(solution)/shard_map/ppermute | solution.py:108
  3.7 113.4 %collective-permute-start.35 = (bf16[64,2048]{1,0:T(8,128)(2,1)}, bf16[64,2048]{1,0:T(8,128)(2,1)}, u32[]{:S(2)}, u32[]{:S(2)}) collective-permute-start(bf16[64,2048]{1,0:T(8,128)(2,1)} %bitcast.118), channel_id=1, source_target_pairs={{0,4},{2,6},{4,0},{6,2},{8,12},{10,14},{12,8},{14,10},{16,20},{18,... | collective-permute-start | bytes 786440 | tf_op jit(solution)/shard_map/ppermute | solution.py:108
  24.2 48.5 %collective-permute-start.24 = (bf16[64,2048]{1,0:T(8,128)(2,1)}, bf16[64,2048]{1,0:T(8,128)(2,1)}, u32[]{:S(2)}, u32[]{:S(2)}) collective-permute-start(bf16[64,2048]{1,0:T(8,128)(2,1)} %param.20), channel_id=1, source_target_pairs={{0,8},{2,10},{4,12},{6,14},{8,16},{10,18},{12,20},{14,22},{16,24},... | collective-permute-start | bytes 786440 | tf_op jit(solution)/shard_map/ppermute | solution.py:108
  24.8 40.1 %collective-permute-start.7 = (bf16[64,1536]{1,0:T(8,128)(2,1)S(1)}, bf16[64,1536]{1,0:T(8,128)(2,1)S(1)}, u32[]{:S(2)}, u32[]{:S(2)}) collective-permute-start(bf16[64,1536]{1,0:T(8,128)(2,1)S(1)} %bitcast.112), channel_id=1, source_target_pairs={{0,8},{2,10},{4,12},{6,14},{8,16},{10,18},{12,20},{14,22},{16,24},... | collective-permute-start | bytes 589832 | tf_op jit(solution)/shard_map/ppermute | solution.py:108
  63.7 82.3 %collective-permute-start.27 = (bf16[64,2048]{1,0:T(8,128)(2,1)}, bf16[64,2048]{1,0:T(8,128)(2,1)S(1)}, u32[]{:S(2)}, u32[]{:S(2)}) collective-permute-start(bf16[64,2048]{1,0:T(8,128)(2,1)} %param.20), channel_id=1, source_target_pairs={{0,4},{2,6},{4,0},{6,2},{8,12},{10,14},{12,8},{14,10},{16,20},{18,... | collective-permute-start | bytes 786440 | tf_op jit(solution)/shard_map/ppermute | solution.py:108
  82.3 21.5 %collective-permute-start.10 = (bf16[64,1536]{1,0:T(8,128)(2,1)S(1)}, bf16[64,1536]{1,0:T(8,128)(2,1)S(1)}, u32[]{:S(2)}, u32[]{:S(2)}) collective-permute-start(bf16[64,1536]{1,0:T(8,128)(2,1)S(1)} %bitcast.113), channel_id=1, source_target_pairs={{0,4},{2,6},{4,0},{6,2},{8,12},{10,14},{12,8},{14,10},{16,20},{18,... | collective-permute-start | bytes 589832 | tf_op jit(solution)/shard_map/ppermute | solution.py:108
  103.8 50.2 %collective-permute-start.22 = (bf16[512,512]{1,0:T(8,128)(2,1)S(1)}, bf16[512,512]{1,0:T(8,128)(2,1)S(1)}, u32[]{:S(2)}, u32[]{:S(2)}) collective-permute-start(bf16[512,512]{1,0:T(8,128)(2,1)S(1)} %copy-done.44), channel_id=1, source_target_pairs={{0,2},{2,0},{4,6},{6,4},{8,10},{10,8},{12,14},{14,12},{16,18},{18,... | collective-permute-start | bytes 1572872 | tf_op jit(solution)/shard_map/ppermute | solution.py:108
  115.6 32.0 %collective-permute-start.28 = (bf16[64,2048]{1,0:T(8,128)(2,1)}, bf16[64,2048]{1,0:T(8,128)(2,1)S(1)}, u32[]{:S(2)}, u32[]{:S(2)}) collective-permute-start(bf16[64,2048]{1,0:T(8,128)(2,1)} %collective-permute-done.24), channel_id=1, source_target_pairs={{0,4},{2,6},{4,0},{6,2},{8,12},{10,14},{12,8},{14,10},{16,20},{18,... | collective-permute-start | bytes 786440 | tf_op jit(solution)/shard_map/ppermute | solution.py:108
  135.0 27.0 %collective-permute-start.14 = (bf16[512,1536]{1,0:T(8,128)(2,1)S(1)}, bf16[512,1536]{1,0:T(8,128)(2,1)S(1)}, u32[]{:S(2)}, u32[]{:S(2)}) collective-permute-start(bf16[512,1536]{1,0:T(8,128)(2,1)S(1)} %get-tuple-element.141), channel_id=1, source_target_pairs={{0,2},{2,0},{4,6},{6,4},{8,10},{10,8},{12,14},{14,12},{16,18},{18,... | collective-permute-start | bytes 4718600 | tf_op jit(solution)/shard_map/ppermute | solution.py:108
  162.0 20.0 %collective-permute-start.31 = (bf16[512,2048]{1,0:T(8,128)(2,1)}, bf16[512,2048]{1,0:T(8,128)(2,1)}, u32[]{:S(2)}, u32[]{:S(2)}) collective-permute-start(bf16[512,2048]{1,0:T(8,128)(2,1)} %get-tuple-element.109), channel_id=1, source_target_pairs={{0,2},{2,0},{4,6},{6,4},{8,10},{10,8},{12,14},{14,12},{16,18},{18,... | collective-permute-start | bytes 6291464 | tf_op jit(solution)/shard_map/ppermute | solution.py:108
  173.7 25.7 %collective-permute-start.23 = (bf16[512,1024]{1,0:T(8,128)(2,1)S(1)}, bf16[512,1024]{1,0:T(8,128)(2,1)}, u32[]{:S(2)}, u32[]{:S(2)}) collective-permute-start(bf16[512,1024]{1,0:T(8,128)(2,1)S(1)} %convolution_convert_fusion), channel_id=1, source_target_pairs={{0,1},{1,0},{2,3},{3,2},{4,5},{5,4},{6,7},{7,6},{8,9},{9,8},{10,11... | collective-permute-start | bytes 3145736 | tf_op jit(solution)/shard_map/ppermute | solution.py:174
  218.2 39.6 %collective-permute-start.42 = (bf16[512,1024]{1,0:T(8,128)(2,1)}, bf16[512,1024]{1,0:T(8,128)(2,1)}, u32[]{:S(2)}, u32[]{:S(2)}) collective-permute-start(bf16[512,1024]{1,0:T(8,128)(2,1)} %get-tuple-element.186), channel_id=1, source_target_pairs={{0,1},{1,0},{2,3},{3,2},{4,5},{5,4},{6,7},{7,6},{8,9},{9,8},{10,11... | collective-permute-start | bytes 3145736 | tf_op jit(solution)/shard_map/ppermute | solution.py:174
  221.0 33.6 %collective-permute-start.40 = (bf16[256,1024]{1,0:T(8,128)(2,1)}, bf16[256,1024]{1,0:T(8,128)(2,1)}, u32[]{:S(2)}, u32[]{:S(2)}) collective-permute-start(bf16[256,1024]{1,0:T(8,128)(2,1)} %constant_dynamic-slice_fusion.3), channel_id=1, source_target_pairs={{0,1},{1,0},{2,3},{3,2},{4,5},{5,4},{6,7},{7,6},{8,9},{9,8},{10,11... | collective-permute-start | bytes 1572872 | tf_op jit(solution)/shard_map/ppermute | solution.py:174
  223.3 138.6 %collective-permute-start.60 = (bf16[512,2048]{1,0:T(8,128)(2,1)}, bf16[512,2048]{1,0:T(8,128)(2,1)}, u32[]{:S(2)}, u32[]{:S(2)}) collective-permute-start(bf16[512,2048]{1,0:T(8,128)(2,1)} %slice.497), channel_id=1, source_target_pairs={{0,2},{2,0},{4,6},{6,4},{8,10},{10,8},{12,14},{14,12},{16,18},{18,... | collective-permute-start | bytes 6291464 | tf_op jit(solution)/shard_map/ppermute | solution.py:108
  230.9 138.4 %collective-permute-start.68 = (bf16[512,2048]{1,0:T(8,128)(2,1)}, bf16[512,2048]{1,0:T(8,128)(2,1)}, u32[]{:S(2)}, u32[]{:S(2)}) collective-permute-start(bf16[512,2048]{1,0:T(8,128)(2,1)} %slice.496), channel_id=1, source_target_pairs={{0,2},{2,0},{4,6},{6,4},{8,10},{10,8},{12,14},{14,12},{16,18},{18,... | collective-permute-start | bytes 6291464 | tf_op jit(solution)/shard_map/ppermute | solution.py:108
  337.1 59.2 %collective-permute-start.44 = (bf16[512,1536]{1,0:T(8,128)(2,1)}, bf16[512,1536]{1,0:T(8,128)(2,1)S(1)}, u32[]{:S(2)}, u32[]{:S(2)}) collective-permute-start(bf16[512,1536]{1,0:T(8,128)(2,1)} %slice.498), channel_id=1, source_target_pairs={{0,2},{2,0},{4,6},{6,4},{8,10},{10,8},{12,14},{14,12},{16,18},{18,... | collective-permute-start | bytes 4718600 | tf_op jit(solution)/shard_map/ppermute | solution.py:108
  367.3 32.7 %collective-permute-start.63 = (bf16[64,2048]{1,0:T(8,128)(2,1)S(1)}, bf16[64,2048]{1,0:T(8,128)(2,1)S(1)}, u32[]{:S(2)}, u32[]{:S(2)}) collective-permute-start(bf16[64,2048]{1,0:T(8,128)(2,1)S(1)} %get-tuple-element.90), channel_id=1, source_target_pairs={{0,4},{2,6},{4,0},{6,2},{8,12},{10,14},{12,8},{14,10},{16,20},{18,... | collective-permute-start | bytes 786440 | tf_op jit(solution)/shard_map/ppermute | solution.py:108
  367.9 56.5 %collective-permute-start.62 = (bf16[64,2048]{1,0:T(8,128)(2,1)S(1)}, bf16[64,2048]{1,0:T(8,128)(2,1)S(1)}, u32[]{:S(2)}, u32[]{:S(2)}) collective-permute-start(bf16[64,2048]{1,0:T(8,128)(2,1)S(1)} %get-tuple-element.91), channel_id=1, source_target_pairs={{0,4},{2,6},{4,0},{6,2},{8,12},{10,14},{12,8},{14,10},{16,20},{18,... | collective-permute-start | bytes 786440 | tf_op jit(solution)/shard_map/ppermute | solution.py:108
  369.3 83.3 %collective-permute-start.61 = (bf16[64,2048]{1,0:T(8,128)(2,1)S(1)}, bf16[64,2048]{1,0:T(8,128)(2,1)S(1)}, u32[]{:S(2)}, u32[]{:S(2)}) collective-permute-start(bf16[64,2048]{1,0:T(8,128)(2,1)S(1)} %get-tuple-element.88), channel_id=1, source_target_pairs={{0,4},{2,6},{4,0},{6,2},{8,12},{10,14},{12,8},{14,10},{16,20},{18,... | collective-permute-start | bytes 786440 | tf_op jit(solution)/shard_map/ppermute | solution.py:108
  399.9 34.2 %collective-permute-start.70 = (bf16[64,2048]{1,0:T(8,128)(2,1)S(1)}, bf16[64,2048]{1,0:T(8,128)(2,1)S(1)}, u32[]{:S(2)}, u32[]{:S(2)}) collective-permute-start(bf16[64,2048]{1,0:T(8,128)(2,1)S(1)} %get-tuple-element.87), channel_id=1, source_target_pairs={{0,4},{2,6},{4,0},{6,2},{8,12},{10,14},{12,8},{14,10},{16,20},{18,... | collective-permute-start | bytes 786440 | tf_op jit(solution)/shard_map/ppermute | solution.py:108
  408.8 59.6 %collective-permute-start.69 = (bf16[64,2048]{1,0:T(8,128)(2,1)S(1)}, bf16[64,2048]{1,0:T(8,128)(2,1)S(1)}, u32[]{:S(2)}, u32[]{:S(2)}) collective-permute-start(bf16[64,2048]{1,0:T(8,128)(2,1)S(1)} %get-tuple-element.84), channel_id=1, source_target_pairs={{0,4},{2,6},{4,0},{6,2},{8,12},{10,14},{12,8},{14,10},{16,20},{18,... | collective-permute-start | bytes 786440 | tf_op jit(solution)/shard_map/ppermute | solution.py:108
  424.4 20.7 %collective-permute-start.47 = (bf16[64,1536]{1,0:T(8,128)(2,1)S(1)}, bf16[64,1536]{1,0:T(8,128)(2,1)S(1)}, u32[]{:S(2)}, u32[]{:S(2)}) collective-permute-start(bf16[64,1536]{1,0:T(8,128)(2,1)S(1)} %get-tuple-element.94), channel_id=1, source_target_pairs={{0,4},{2,6},{4,0},{6,2},{8,12},{10,14},{12,8},{14,10},{16,20},{18,... | collective-permute-start | bytes 589832 | tf_op jit(solution)/shard_map/ppermute | solution.py:108
  434.2 27.5 %collective-permute-start.46 = (bf16[64,1536]{1,0:T(8,128)(2,1)S(1)}, bf16[64,1536]{1,0:T(8,128)(2,1)S(1)}, u32[]{:S(2)}, u32[]{:S(2)}) collective-permute-start(bf16[64,1536]{1,0:T(8,128)(2,1)S(1)} %get-tuple-element.95), channel_id=1, source_target_pairs={{0,4},{2,6},{4,0},{6,2},{8,12},{10,14},{12,8},{14,10},{16,20},{18,... | collective-permute-start | bytes 589832 | tf_op jit(solution)/shard_map/ppermute | solution.py:108
  445.1 24.1 %collective-permute-start.45 = (bf16[64,1536]{1,0:T(8,128)(2,1)S(1)}, bf16[64,1536]{1,0:T(8,128)(2,1)S(1)}, u32[]{:S(2)}, u32[]{:S(2)}) collective-permute-start(bf16[64,1536]{1,0:T(8,128)(2,1)S(1)} %get-tuple-element.92), channel_id=1, source_target_pairs={{0,4},{2,6},{4,0},{6,2},{8,12},{10,14},{12,8},{14,10},{16,20},{18,... | collective-permute-start | bytes 589832 | tf_op jit(solution)/shard_map/ppermute | solution.py:108
  (118 other events, 1719.3 us)
